TPU v7x, 32 devices: a whole 2x2x4 slice. The times are simulated.
32 devices in a mesh: pool: 2 (over x), node: 16 (over z, y, core), local: 1.
Axes of the slice: x: 2, y: 2, z: 4, core: 2. Of those that a mesh axis runs over, the one named last changes fastest.
Arguments:
- tokens: bfloat16 [512, 3584], P(('pool', 'node', 'local')), parts along dimension 0, may hold values from -6 to 6
- routes: int32 [512, 8], P(('pool', 'node', 'local')), parts along dimension 0, may hold values from 0 to 15, all different within a row; in each aligned block of 16 rows (0 to 15, 16 to 31, ...) at most 16 rows name the same one
- route_weights: int32 [512, 8], P(('pool', 'node', 'local')), parts along dimension 0, may hold values from 1 to 256
- placement: int32 [16], replicated, may hold values from 0 to 15, each once
- expert_gate: bfloat16 [16, 3584, 1024], P('node', None, 'local'), may hold values from -0.09375 to 0.09375
- expert_up: bfloat16 [16, 3584, 1024], P('node', None, 'local'), may hold values from -0.09375 to 0.09375
- expert_down: bfloat16 [16, 1024, 3584], P('node', 'local'), may hold values from -0.1875 to 0.1875
- shared_gate: bfloat16 [3584, 2048], P(None, 'node'), may hold values from -0.09375 to 0.09375
- shared_up: bfloat16 [3584, 2048], P(None, 'node'), may hold values from -0.09375 to 0.09375
- shared_down: bfloat16 [2048, 3584], P('node'), may hold values from -0.125 to 0.125
Outputs:
- mixed: bfloat16 [512, 3584], P(('pool', 'node', 'local')), parts along dimension 0
There are 2 independent parts, one for each index of `pool`. A program takes and returns all parts, laid end to end along the dimension named above; an argument that names none is the same for every part. Nothing has to cross between parts.
Inputs may be any that keep to these rules, and one draw needn't show every extreme that they name: `routes`: each row names 8 different experts; the 16 rows of one device name one expert at most 16 times, a bound that some block reaches in some devices' rows. `placement`: each slot holds exactly one expert.
All inputs are finite; a program needn't handle non-finite values.
Results may differ from a plain program's by a relative error of at most 0.015.
Values may be sent and summed in bfloat16 or wider, within the bound.
No kernel may reach another device: no remote copies, remote signals or barrier semaphores. Data moves between devices by JAX's collectives and lax.ppermute only.
A program may use at most 128 MiB of HBM per device.

v0:
```python
import jax
import jax.numpy as jnp
from jax import lax
from jax.sharding import PartitionSpec as P

TOPK = 8


gain_scale = 1.0 / 256.0


def shards(
    tokens,
    routes,
    route_weights,
    placement,
    expert_gate,
    expert_up,
    expert_down,
    shared_gate,
    shared_up,
    shared_down,
):
    node_count = lax.axis_size("node")
    core_count = lax.axis_size("local")
    tok_count = tokens.shape[0]
    model_width = tokens.shape[1]
    capacity = min(tok_count, 2 * tok_count * TOPK // node_count)
    pair_count = tok_count * TOPK
    slot_count = node_count * capacity
    expert_index = routes.reshape(pair_count)
    expert_onehot = (
        expert_index[:, None] == jnp.arange(node_count, dtype=jnp.int32)[None, :]
    ).astype(jnp.int32)
    chip_index = jnp.sum(expert_onehot * placement[None, :], axis=1)
    chip_onehot = (chip_index[:, None] == jnp.arange(node_count, dtype=jnp.int32)[None, :]).astype(
        jnp.int32
    )
    before = jnp.cumsum(chip_onehot, axis=0) - chip_onehot
    slot_rank = jnp.sum(before * chip_onehot, axis=1)
    slot_index = chip_index * capacity + slot_rank
    slot_onehot = (slot_index[:, None] == jnp.arange(slot_count, dtype=jnp.int32)[None, :]).astype(
        jnp.float32
    )
    token_of_pair = jnp.arange(pair_count, dtype=jnp.int32) // TOPK
    token_onehot = (
        token_of_pair[:, None] == jnp.arange(tok_count, dtype=jnp.int32)[None, :]
    ).astype(jnp.float32)
    picker = jnp.dot(slot_onehot.T, token_onehot).astype(jnp.bfloat16)
    outgoing = jnp.dot(picker, tokens, preferred_element_type=jnp.float32).astype(jnp.bfloat16)
    outgoing = outgoing.reshape(node_count, capacity, model_width)
    gains = route_weights.reshape(pair_count).astype(jnp.float32) * gain_scale
    combine = jnp.dot(token_onehot.T, slot_onehot * gains[:, None]).astype(jnp.bfloat16)
    doubled = jnp.broadcast_to(outgoing[:, None], (node_count, core_count, capacity, model_width))
    doubled = doubled.reshape(node_count * core_count, capacity, model_width)
    arrived = lax.all_to_all(doubled, ("node", "local"), split_axis=0, concat_axis=0, tiled=True)
    gathered = arrived.reshape(node_count * core_count * capacity, model_width)
    gate_act = jnp.dot(gathered, expert_gate[0], preferred_element_type=jnp.float32)
    up_act = jnp.dot(gathered, expert_up[0], preferred_element_type=jnp.float32)
    hidden = (jax.nn.silu(gate_act) * up_act).astype(jnp.bfloat16)
    partial_rows = jnp.dot(hidden, expert_down[0], preferred_element_type=jnp.float32).astype(
        jnp.bfloat16
    )
    partial_rows = partial_rows.reshape(node_count * core_count, capacity, model_width)
    came_back = lax.all_to_all(
        partial_rows, ("node", "local"), split_axis=0, concat_axis=0, tiled=True
    )
    came_back = came_back.reshape(node_count, core_count, capacity, model_width).astype(jnp.float32)
    returned_rows = jnp.sum(came_back, axis=1).astype(jnp.bfloat16)
    routed = jnp.dot(
        combine, returned_rows.reshape(slot_count, model_width), preferred_element_type=jnp.float32
    )
    shard_rows = lax.all_gather(tokens, "node", axis=0, tiled=True)
    gate_act = jnp.dot(shard_rows, shared_gate, preferred_element_type=jnp.float32)
    up_act = jnp.dot(shard_rows, shared_up, preferred_element_type=jnp.float32)
    hidden = (jax.nn.silu(gate_act) * up_act).astype(jnp.bfloat16)
    shared_terms = jnp.dot(hidden, shared_down, preferred_element_type=jnp.float32)
    shared = lax.psum_scatter(
        shared_terms.astype(jnp.bfloat16), "node", scatter_dimension=0, tiled=True
    ).astype(jnp.float32)
    return (routed + shared).astype(jnp.bfloat16)


def solution(mesh):
    placed = (
        P(("pool", "node", "local"), None),
        P(("pool", "node", "local"), None),
        P(("pool", "node", "local"), None),
        P(),
        P("node", None, "local"),
        P("node", None, "local"),
        P("node", "local", None),
        P(None, "node"),
        P(None, "node"),
        P("node", None),
    )
    return jax.shard_map(
        shards,
        mesh=mesh,
        in_specs=placed,
        out_specs=P(("pool", "node", "local"), None),
        check_vma=False,
    )
```

profile of v0, /device:TPU:0, one launch (start us, length us, event | category | flops | bytes accessed | tf_op | source)
XLA Modules:
  0.0 171.5 jit_solution(17432023763214995863)
XLA Ops:
  6.5 0.0 copy-start
  6.5 0.8 copy.13
  7.4 0.1 eq.63
  7.5 0.8 select_reduce_fusion.1
  8.3 0.1 fusion.36
  8.4 0.2 reduce_window_sum.11
  8.6 0.2 select_reduce_fusion
  8.8 3.0 %convolution_convert_fusion.1 = bf16[256,3584]{1,0:T(8,128)(2,1)} fusion(bf16[16,3584]{1,0:T(8,128)(2,1)} %param.10, s32[128]{0:T(128)S(1)} %get-tuple-element.6, s32[128]{0:T(128)S(1)} %get-tuple-element.5), kind=kOutput, calls=%fused_computation.8 | convolution fusion | flops 31365120 | bytes 1950720 | tf_op jit(solution)/shard_map/dot_general | solution.py:50
  11.8 7.4 %all-to-all-start = ((bf16[16,16,3584]{2,1,0:T(8,128)(2,1)}), bf16[16,16,3584]{2,1,0:T(8,128)(2,1)S(1)}, u32[]{:S(2)}, u32[]{:S(2)}) async-start(bf16[16,16,3584]{2,1,0:T(8,128)(2,1)} %bitcast), calls=%async_computation | async-start | bytes 3670016 | tf_op jit(solution)/shard_map/all_to_all | solution.py:56
  19.2 0.0 all-gather.2.cloned.1.call-start
  19.2 0.7 all-gather.2.cloned.1.call-update
  19.9 39.4 %all-to-all-done = bf16[16,16,3584]{2,1,0:T(8,128)(2,1)S(1)} async-done(((bf16[16,16,3584]{2,1,0:T(8,128)(2,1)}), bf16[16,16,3584]{2,1,0:T(8,128)(2,1)S(1)}, u32[]{:S(2)}, u32[]{:S(2)}) %all-to-all-start) | async-done | bytes 1835040 | tf_op jit(solution)/shard_map/all_to_all | solution.py:56
  59.3 6.1 %fusion.4 = f32[256,1024]{1,0:T(8,128)} fusion(bf16[256,3584]{1,0:T(8,128)(2,1)S(1)} %bitcast.32, bf16[1,3584,1024]{2,1,0:T(8,128)(2,1)} %param.14), kind=kOutput, calls=%fused_computation.4 | convolution fusion | flops 1879048192 | bytes 10223616 | tf_op jit(solution)/shard_map/dot_general | solution.py:58
  65.4 10.8 %fusion.6 = bf16[256,3584]{1,0:T(8,128)(2,1)} fusion(bf16[1,1024,3584]{2,1,0:T(8,128)(2,1)} %param.16, bf16[256,3584]{1,0:T(8,128)(2,1)S(1)} %bitcast.33, bf16[1,3584,1024]{2,1,0:T(8,128)(2,1)} %param.15, f32[256,1024]{1,0:T(8,128)} %fusion.4), kind=kOutput, calls=%fused_computation.6 | convolution fusion | flops 3760586752 | bytes 19398656 | tf_op jit(solution)/shard_map/dot_general | solution.py:61
  76.2 17.1 %all-to-all-start.1 = ((bf16[16,16,3584]{2,1,0:T(8,128)(2,1)}), bf16[16,16,3584]{2,1,0:T(8,128)(2,1)S(1)}, u32[]{:S(2)}, u32[]{:S(2)}) async-start(bf16[16,16,3584]{2,1,0:T(8,128)(2,1)} %bitcast.31), calls=%async_computation.1 | async-start | bytes 3670016 | tf_op jit(solution)/shard_map/all_to_all | solution.py:65
  93.4 0.0 reduce-scatter.2.cloned.1.call-start
  93.4 0.0 all-gather.2.cloned.1.call-done
  93.4 2.4 %fusion.45 = f32[256,128]{1,0:T(8,128)S(1)} fusion(bf16[256,3584]{1,0:T(8,128)(2,1)} %all-gather.2.cloned.1.call-done, bf16[3584,128]{1,0:T(8,128)(2,1)} %param.17), kind=kOutput, calls=%fused_computation.47 | convolution fusion | flops 234881024 | bytes 2883584 | tf_op jit(solution)/shard_map/dot_general | solution.py:74
  95.8 0.0 copy-done
  95.8 4.2 %convolution_convert_fusion = bf16[256,3584]{1,0:T(8,128)(2,1)} fusion(bf16[128,3584]{1,0:T(8,128)(2,1)S(1)} %copy-done, bf16[256,3584]{1,0:T(8,128)(2,1)} %all-gather.2.cloned.1.call-done, bf16[3584,128]{1,0:T(8,128)(2,1)} %param.18, f32[256,128]{1,0:T(8,128)S(1)} %fusion.45), kind=kOutput, calls=%fused_computation.7 | convolution fusion | flops 470876160 | bytes 5636096 | tf_op jit(solution)/shard_map/dot_general | solution.py:77
  100.0 0.0 copy-start.1
  100.0 0.0 reduce-scatter.2.cloned.1.call-update
  100.0 0.7 copy-done.1
  100.7 0.1 copy.14
  100.7 0.1 mul.63
  100.8 61.7 %reduce-scatter.2.cloned.1.call-done = bf16[16,3584]{1,0:T(8,128)(2,1)} async-done(((bf16[256,3584]{1,0:T(8,128)(2,1)}), bf16[16,3584]{1,0:T(8,128)(2,1)}) %reduce-scatter.2.cloned.1.call-update) | async-done | bytes 114704 | tf_op jit(solution)/shard_map/reduce_scatter | solution.py:78
  162.5 0.0 all-to-all-done.1
  162.5 2.1 %fusion.9 = bf16[16,3584]{1,0:T(8,128)(2,1)} fusion(bf16[256,3584]{1,0:T(8,128)(2,1)S(1)} %bitcast.30, bf16[16,3584]{1,0:T(8,128)(2,1)} %reduce-scatter.2.cloned.1.call-done, bf16[128]{0:T(256)(128)(2,1)S(1)} %mul.63, s32[128]{0:T(128)S(1)} %get-tuple-element.6, s32[128]{0:T(128)S(1)} %get-tuple-element.5), kind=kOutput, calls=%fused_computation.10 | convolution fusion | flops 30648320 | bytes 2065664 | tf_op jit(solution)/shard_map/dot_general | solution.py:70
  (2 shorter events, 0.0 us)
Async XLA Ops:
  6.5 89.3 %copy-start = (bf16[128,3584]{1,0:T(8,128)(2,1)S(1)}, bf16[128,3584]{1,0:T(8,128)(2,1)}, u32[]{:S(2)}) copy-start(bf16[128,3584]{1,0:T(8,128)(2,1)} %param.19) | copy-start | bytes 2752516
  11.8 47.5 %all-to-all-start = ((bf16[16,16,3584]{2,1,0:T(8,128)(2,1)}), bf16[16,16,3584]{2,1,0:T(8,128)(2,1)S(1)}, u32[]{:S(2)}, u32[]{:S(2)}) async-start(bf16[16,16,3584]{2,1,0:T(8,128)(2,1)} %bitcast), calls=%async_computation | async-start | bytes 3670016 | tf_op jit(solution)/shard_map/all_to_all | solution.py:56
  19.2 74.2 %all-gather.2.cloned.1.call-start = ((), (), s32[]{:S(2)}) async-start(), calls=%async_computation.3 | async-start | bytes 1949696 | tf_op jit(solution)/shard_map/all_gather | solution.py:73
  76.2 86.3 %all-to-all-start.1 = ((bf16[16,16,3584]{2,1,0:T(8,128)(2,1)}), bf16[16,16,3584]{2,1,0:T(8,128)(2,1)S(1)}, u32[]{:S(2)}, u32[]{:S(2)}) async-start(bf16[16,16,3584]{2,1,0:T(8,128)(2,1)} %bitcast.31), calls=%async_computation.1 | async-start | bytes 3670016 | tf_op jit(solution)/shard_map/all_to_all | solution.py:65
  93.4 69.2 %reduce-scatter.2.cloned.1.call-start = ((), (), s32[]{:S(2)}) async-start(), calls=%async_computation.4 | async-start | bytes 1949696 | tf_op jit(solution)/shard_map/reduce_scatter | solution.py:78
  100.0 0.7 copy-start.1
Sparse Core Ops, SparseCore 0:
  22.3 52.7 all-gather.1
  100.1 62.3 reduce-scatter.1
where the time goes:
time: 172 us
  waiting for transfers between devices  102 us (59%)
  matrix products  28.6 us (17%)
  starting transfers between devices  24.6 us (14%)
  between operations  13.5 us (8%)
  local copies, waits for them, and re-layouts  1.77 us (1%)
    reduce_scatter x1, waiting for transfers between devices, shards(): lax.psum_scatter(shared_terms.astype(jnp.bfloat16), 'node', scatter_dimen...  61.7 us
    all_to_all x1, waiting for transfers between devices, shards(): lax.all_to_all(doubled, ('node', 'local'), split_axis=0, concat_axis=0, t...  39.4 us
    all_to_all x1, starting transfers between devices, shards(): lax.all_to_all(partial_rows, ('node', 'local'), split_axis=0, concat_axis...  17.1 us
    dot_general x1, matrix products, shards(): jnp.dot(hidden, expert_down[0], preferred_element_type=jnp.float32)  10.8 us
    all_to_all x1, starting transfers between devices, shards(): lax.all_to_all(doubled, ('node', 'local'), split_axis=0, concat_axis=0, t...  7.41 us
    dot_general x1, matrix products, shards(): jnp.dot(gathered, expert_gate[0], preferred_element_type=jnp.float32)  6.11 us
    dot_general x1, matrix products, shards(): jnp.dot(hidden, shared_down, preferred_element_type=jnp.float32)  4.16 us
  transfers between devices with their start and end apart: 4, of which 2 were waited for; matrix products, arithmetic and copies ran while one was open for 14% of the time, Pallas kernels for 0%

commit v1 on v0

v1 whole, which is shorter than its diff:
```python
import jax
import jax.numpy as jnp
from jax import lax
from jax.sharding import PartitionSpec as P

gain_scale = 1.0 / 256.0
LANES = 128


def peers(flip, count):
    return [(device, device ^ flip) for device in range(count)]


def shards(
    tokens,
    routes,
    route_weights,
    placement,
    expert_gate,
    expert_up,
    expert_down,
    shared_gate,
    shared_up,
    shared_down,
):
    node_count = lax.axis_size("node")
    core_count = lax.axis_size("local")
    tok_count, model_width = tokens.shape
    device_count = node_count * core_count
    assert device_count & (device_count - 1) == 0
    flips = [1 << bit for bit in range(device_count.bit_length() - 1)]
    inner = max(1, core_count.bit_length() - 1)
    axes = ("node", "local")

    def swap(rows, flip):
        return lax.ppermute(rows, axes, peers(flip, device_count))

    slots = lax.broadcasted_iota(jnp.int32, (1, 1, node_count), 2)
    chip_slot = jnp.sum(
        jnp.where(routes[:, :, None] == slots, placement[None, None, :], 0), axis=2
    )
    gains = jnp.sum(
        jnp.where(
            chip_slot[:, :, None] == slots,
            route_weights.astype(jnp.float32)[:, :, None] * gain_scale,
            0.0,
        ),
        axis=1,
    ).astype(jnp.bfloat16)
    gain_width = -(-node_count // LANES) * LANES
    gains = jnp.pad(gains, ((0, 0), (0, gain_width - node_count)))
    own = jnp.concatenate([tokens, gains], axis=1)

    axis_y, axis_l, axis_h = flips[inner : inner + 3]
    rest = flips[inner + 3 :] + flips[:inner]
    row_y, row_l, row_h = swap(own, axis_y), swap(own, axis_l), swap(own, axis_h)
    row_lh = swap(row_h, axis_l)
    row_ly_hy = swap(jnp.concatenate([row_l, row_h]), axis_y)
    row_lhy = swap(row_lh, axis_y)
    rows = jnp.concatenate([own, row_y, row_l, row_h, row_lh, row_ly_hy, row_lhy])
    for flip in rest:
        rows = jnp.concatenate([rows, swap(rows, flip)])

    x = rows[:, :model_width]
    slot = lax.axis_index("node")
    my_gain = jnp.sum(
        jnp.where(
            lax.broadcasted_iota(jnp.int32, (1, gain_width), 1) == slot,
            rows[:, model_width:].astype(jnp.float32),
            0.0,
        ),
        axis=1,
        keepdims=True,
    )
    gate_act = jnp.dot(x, expert_gate[0], preferred_element_type=jnp.float32)
    up_act = jnp.dot(x, expert_up[0], preferred_element_type=jnp.float32)
    hidden = (jax.nn.silu(gate_act) * up_act * my_gain).astype(jnp.bfloat16)
    shared_gate_act = jnp.dot(x, shared_gate, preferred_element_type=jnp.float32)
    shared_up_act = jnp.dot(x, shared_up, preferred_element_type=jnp.float32)
    shared_hidden = jax.nn.silu(shared_gate_act) * shared_up_act
    if core_count > 1:
        row = lax.broadcasted_iota(jnp.int32, (rows.shape[0], 1), 0)
        shared_hidden = jnp.where(row < tok_count * node_count, shared_hidden, 0.0)
    shared_hidden = shared_hidden.astype(jnp.bfloat16)
    parts = jnp.dot(hidden, expert_down[0], preferred_element_type=jnp.float32)
    parts += jnp.dot(shared_hidden, shared_down, preferred_element_type=jnp.float32)

    def wide(rows):
        return rows.astype(jnp.float32)

    def narrow(rows):
        return rows.astype(jnp.bfloat16)

    sums = parts
    for flip in reversed(rest):
        half = sums.shape[0] // 2
        sums = sums[:half] + wide(swap(narrow(sums[half:]), flip))
    own, sum_y, sum_l, sum_h, sum_lh, sum_ly, sum_hy, sum_lhy = jnp.split(sums, 8)
    sum_lh += wide(swap(narrow(sum_lhy), axis_y))
    back = wide(swap(narrow(jnp.concatenate([sum_ly, sum_hy])), axis_y))
    sum_l += back[:tok_count]
    sum_h += back[tok_count:]
    sum_h += wide(swap(narrow(sum_lh), axis_l))
    own += wide(swap(narrow(sum_y), axis_y))
    own += wide(swap(narrow(sum_l), axis_l))
    own += wide(swap(narrow(sum_h), axis_h))
    return narrow(own)


def solution(mesh):
    placed = (
        P(("pool", "node", "local"), None),
        P(("pool", "node", "local"), None),
        P(("pool", "node", "local"), None),
        P(),
        P("node", None, "local"),
        P("node", None, "local"),
        P("node", "local", None),
        P(None, "node"),
        P(None, "node"),
        P("node", None),
    )
    return jax.shard_map(
        shards,
        mesh=mesh,
        in_specs=placed,
        out_specs=P(("pool", "node", "local"), None),
        check_vma=False,
    )
```

time: 172 us -> 80.8 us (0.47)
  waiting for transfers between devices: 102 us -> 26.7 us
  between operations: 13.5 us -> 0.09 us
  starting transfers between devices: 24.6 us -> 16.1 us
  local copies, waits for them, and re-layouts: 1.77 us -> 7.79 us
  matrix products: 28.6 us -> 23.4 us
  other arithmetic: 1.27 us -> 6.28 us
    reduce_scatter x1 -> x0, waiting for transfers between devices: 61.7 us -> none  [shards(): lax.psum_scatter(shared_terms.astype(jnp.bfloat16), 'node', scatter_dimen...]
    all_to_all x2 -> x0, waiting for transfers between devices: 39.4 us -> none  [the longest x1 39.4 us: shards(): lax.all_to_all(doubled, ('node', 'local'), split_axis=0, concat_axis=0, t...]
    ppermute x0 -> x14, waiting for transfers between devices: none -> 26.7 us  [swap(): return lax.ppermute(rows, axes, peers(flip, device_count))]
    all_to_all x2 -> x0, starting transfers between devices: 24.5 us -> none  [the longest x1 17.1 us: shards(): lax.all_to_all(partial_rows, ('node', 'local'), split_axis=0, concat_axis...]
    ppermute x0 -> x14, starting transfers between devices: none -> 16.1 us  [swap(): return lax.ppermute(rows, axes, peers(flip, device_count))]
    dot_general x6 -> x4, matrix products: 28.6 us -> 23.4 us  [the longest x1 11.3 us: shards(): parts = jnp.dot(hidden, expert_down[0], preferred_element_type=jnp.float32)]
    unnamed x5 -> x10, local copies, waits for them, and re-layouts: 1.5 us -> 4.13 us
    concatenate x0 -> x3, local copies, waits for them, and re-layouts: none -> 1.98 us  [the longest x1 1.3 us: shards(): rows = jnp.concatenate([rows, swap(rows, flip)])]
  transfers between devices with their start and end apart: 4 -> 14, of which waited for: 2 -> 10; matrix products, arithmetic and copies ran while one was open for 14% -> 4% of each run, Pallas kernels for 0% -> 0%
where the time goes in v1:
time: 80.8 us; the launch traced here: 80.4 us
  waiting for transfers between devices  26.7 us (33%)
  matrix products  23.4 us (29%)
  starting transfers between devices  16.1 us (20%)
  local copies, waits for them, and re-layouts  7.79 us (10%)
  other arithmetic  6.28 us (8%)
    ppermute x14, waiting for transfers between devices, swap(): return lax.ppermute(rows, axes, peers(flip, device_count))  26.7 us
    ppermute x14, starting transfers between devices, swap(): return lax.ppermute(rows, axes, peers(flip, device_count))  16.1 us
    dot_general x1, matrix products, shards(): parts = jnp.dot(hidden, expert_down[0], preferred_element_type=jnp.float32)  11.3 us
    dot_general x1, matrix products, shards(): up_act = jnp.dot(x, expert_up[0], preferred_element_type=jnp.float32)  6.11 us
    dot_general x1, matrix products, shards(): jnp.dot(shared_hidden, shared_down, preferred_element_type=jnp.float32)  5.31 us
    unnamed x10, local copies, waits for them, and re-layouts  4.13 us
    another operation x1, other arithmetic  1.76 us
  transfers between devices with their start and end apart: 14, of which 10 were waited for; matrix products, arithmetic and copies ran while one was open for 4% of the time, Pallas kernels for 0%

profile of v1, /device:TPU:0, one launch (start us, length us, event | category | flops | bytes accessed | tf_op | source)
XLA Modules:
  0.0 80.4 jit_solution(15731266593934115974)
XLA Ops:
  0.0 0.8 convert_multiply_fusion
  0.8 0.8 copy.13
  1.6 1.1 %select_reduce_fusion.2 = s32[16,8]{1,0:T(8,128)S(1)} fusion(s32[16]{0:T(128)} %param.13, s32[16,8]{1,0:T(8,128)S(1)} %copy.13), kind=kLoop, calls=%fused_computation.38 | loop fusion | flops 6016 | bytes 1088 | tf_op jit(solution)/shard_map/reduce_sum | solution.py:39
  2.8 1.6 %constant_dynamic-update-slice_fusion.6 = (bf16[128,3712]{1,0:T(8,128)(2,1)}, bf16[16,3712]{1,0:T(8,128)(2,1)S(1)}, bf16[256,3712]{1,0:T(8,128)(2,1)S(1)}) fusion(bf16[16,16]{1,0:T(8,128)(2,1)S(1)} %select_reduce_fusion.1, bf16[16,3584]{1,0:T(8,128)(2,1)} %param.10), kind=kLoop, calls=%fused_computation.46 | loop fusion | flops 356350 | bytes 471552
  4.4 3.1 %collective-permute-start.1 = (bf16[16,3712]{1,0:T(8,128)(2,1)S(1)}, bf16[16,3712]{1,0:T(8,128)(2,1)S(1)}, u32[]{:S(2)}, u32[]{:S(2)}) collective-permute-start(bf16[16,3712]{1,0:T(8,128)(2,1)S(1)} %get-tuple-element.24), channel_id=1, source_target_pairs={{0,4},{1,5},{2,6},{3,7},{4,0},{5,1},{6,2},{7,3},{8,12},{9,13},{10,... | collective-permute-start | bytes 356360 | tf_op jit(solution)/shard_map/ppermute | solution.py:36
  7.4 2.6 %collective-permute-start.2 = (bf16[16,3712]{1,0:T(8,128)(2,1)S(1)}, bf16[16,3712]{1,0:T(8,128)(2,1)S(1)}, u32[]{:S(2)}, u32[]{:S(2)}) collective-permute-start(bf16[16,3712]{1,0:T(8,128)(2,1)S(1)} %get-tuple-element.24), channel_id=1, source_target_pairs={{0,8},{1,9},{2,10},{3,11},{4,12},{5,13},{6,14},{7,15},{8,0},{9,1},... | collective-permute-start | bytes 356360 | tf_op jit(solution)/shard_map/ppermute | solution.py:36
  10.0 1.5 %collective-permute-start = (bf16[16,3712]{1,0:T(8,128)(2,1)S(1)}, bf16[16,3712]{1,0:T(8,128)(2,1)S(1)}, u32[]{:S(2)}, u32[]{:S(2)}) collective-permute-start(bf16[16,3712]{1,0:T(8,128)(2,1)S(1)} %get-tuple-element.24), channel_id=1, source_target_pairs={{0,2},{1,3},{2,0},{3,1},{4,6},{5,7},{6,4},{7,5},{8,10},{9,11},{10,... | collective-permute-start | bytes 356360 | tf_op jit(solution)/shard_map/ppermute | solution.py:36
  12.0 3.7 %collective-permute-done.2 = bf16[16,3712]{1,0:T(8,128)(2,1)S(1)} collective-permute-done((bf16[16,3712]{1,0:T(8,128)(2,1)S(1)}, bf16[16,3712]{1,0:T(8,128)(2,1)S(1)}, u32[]{:S(2)}, u32[]{:S(2)}) %collective-permute-start.2) | collective-permute-done | bytes 118816 | tf_op jit(solution)/shard_map/ppermute | solution.py:36
  15.7 1.6 %collective-permute-start.4 = (bf16[32,3712]{1,0:T(8,128)(2,1)S(1)}, bf16[32,3712]{1,0:T(8,128)(2,1)S(1)}, u32[]{:S(2)}, u32[]{:S(2)}) collective-permute-start(bf16[32,3712]{1,0:T(8,128)(2,1)S(1)} %pad_maximum_fusion), channel_id=1, source_target_pairs={{0,2},{1,3},{2,0},{3,1},{4,6},{5,7},{6,4},{7,5},{8,10},{9,11},{10,... | collective-permute-start | bytes 712712 | tf_op jit(solution)/shard_map/ppermute | solution.py:36
  17.7 0.7 constant_dynamic-update-slice_fusion.5
  18.3 0.7 constant_dynamic-update-slice_fusion.4
  19.0 0.7 constant_dynamic-update-slice_fusion.3
  19.6 2.4 %collective-permute-done.3 = bf16[16,3712]{1,0:T(8,128)(2,1)S(1)} collective-permute-done((bf16[16,3712]{1,0:T(8,128)(2,1)S(1)}, bf16[16,3712]{1,0:T(8,128)(2,1)S(1)}, u32[]{:S(2)}, u32[]{:S(2)}) %collective-permute-start.3) | collective-permute-done | bytes 118816 | tf_op jit(solution)/shard_map/ppermute | solution.py:36
  22.6 0.7 constant_dynamic-update-slice_fusion.2
  23.2 0.7 constant_dynamic-update-slice_fusion.1
  24.0 2.9 %collective-permute-done.5 = bf16[16,3712]{1,0:T(8,128)(2,1)S(1)} collective-permute-done((bf16[16,3712]{1,0:T(8,128)(2,1)S(1)}, bf16[16,3712]{1,0:T(8,128)(2,1)S(1)}, u32[]{:S(2)}, u32[]{:S(2)}) %collective-permute-start.5) | collective-permute-done | bytes 118816 | tf_op jit(solution)/shard_map/ppermute | solution.py:36
  26.9 0.7 constant_dynamic-update-slice_fusion
  27.6 2.8 %collective-permute-done.6 = bf16[128,3712]{1,0:T(8,128)(2,1)} collective-permute-done((bf16[128,3712]{1,0:T(8,128)(2,1)}, bf16[128,3712]{1,0:T(8,128)(2,1)}, u32[]{:S(2)}, u32[]{:S(2)}) %collective-permute-start.6) | collective-permute-done | bytes 950304 | tf_op jit(solution)/shard_map/ppermute | solution.py:36
  30.4 1.3 %constant_dynamic-update-slice_fusion.7 = bf16[256,3712]{1,0:T(8,128)(2,1)S(1)} fusion(bf16[256,3712]{1,0:T(8,128)(2,1)S(1)} %get-tuple-element.14, bf16[128,3712]{1,0:T(8,128)(2,1)} %collective-permute-done.6), kind=kLoop, calls=%fused_computation.47 | loop fusion | bytes 1900544 | tf_op jit(solution)/shard_map/concatenate | solution.py:62
  32.5 6.1 %fusion.2 = f32[256,1024]{1,0:T(8,128)} fusion(bf16[1,3584,1024]{2,1,0:T(8,128)(2,1)} %param.15, bf16[256,3712]{1,0:T(8,128)(2,1)S(1)} %constant_dynamic-update-slice_fusion.7), kind=kOutput, calls=%fused_computation.2 | convolution fusion | flops 1879048192 | bytes 10223616 | tf_op jit(solution)/shard_map/dot_general | solution.py:76
  38.6 11.3 %fusion = f32[256,3584]{1,0:T(8,128)} fusion(bf16[1,1024,3584]{2,1,0:T(8,128)(2,1)} %param.16, f32[256,1024]{1,0:T(8,128)} %fusion.2, bf16[1,3584,1024]{2,1,0:T(8,128)(2,1)} %param.14, bf16[256,3712]{1,0:T(8,128)(2,1)S(1)} %constant_dynamic-update-slice_fusion.7, f32[256]{0:T(256)S(1)} %select_reduce_fusion), kind=kOutput, calls=%fused_computation | convolution fusion | flops 3759931392 | bytes 21234688 | tf_op jit(solution)/shard_map/dot_general | solution.py:85
  50.0 5.3 %convolution_add_fusion = f32[256,3584]{1,0:T(8,128)} fusion(f32[256,3584]{1,0:T(8,128)} %fusion, bf16[128,3584]{1,0:T(8,128)(2,1)S(1)} %copy-done, f32[256,128]{1,0:T(8,128)S(1)} %fusion.6, bf16[3584,128]{1,0:T(8,128)(2,1)} %param.17, bf16[256,3712]{1,0:T(8,128)(2,1)S(1)} %constant_dynamic-update-slice_fusion.7), kind=kOutput, calls=%fused_computation.6 | convolution fusion | flops 470876160 | bytes 11141120 | tf_op jit(solution)/shard_map/dot_general | solution.py:86
  55.3 1.6 %slice.60 = bf16[128,3584]{1,0:T(8,128)(2,1)S(1)} slice(f32[256,3584]{1,0:T(8,128)} %convolution_add_fusion), slice={[128:256], [0:3584]} | slice | bytes 1835008 | tf_op jit(solution)/shard_map/slice | solution.py:97
  57.1 2.3 %collective-permute-done.7 = bf16[128,3584]{1,0:T(8,128)(2,1)S(1)} collective-permute-done((bf16[128,3584]{1,0:T(8,128)(2,1)S(1)}, bf16[128,3584]{1,0:T(8,128)(2,1)S(1)}, u32[]{:S(2)}, u32[]{:S(2)}) %collective-permute-start.7) | collective-permute-done | bytes 917536 | tf_op jit(solution)/shard_map/ppermute | solution.py:36
  59.4 1.8 %fusion.38 = (bf16[128,3584]{1,0:T(8,128)(2,1)S(1)}, f32[128,3584]{1,0:T(8,128)S(1)}) fusion(bf16[128,3584]{1,0:T(8,128)(2,1)S(1)} %collective-permute-done.7, f32[256,3584]{1,0:T(8,128)} %convolution_add_fusion), kind=kLoop, calls=%fused_computation.59 | loop fusion | flops 1376256 | bytes 5505024 | tf_op jit(solution)/shard_map/convert.2
  61.8 1.6 %collective-permute-start.9 = (bf16[32,3584]{1,0:T(8,128)(2,1)S(1)}, bf16[32,3584]{1,0:T(8,128)(2,1)S(1)}, u32[]{:S(2)}, u32[]{:S(2)}) collective-permute-start(bf16[32,3584]{1,0:T(8,128)(2,1)S(1)} %concatenate.21), channel_id=1, source_target_pairs={{0,2},{1,3},{2,0},{3,1},{4,6},{5,7},{6,4},{7,5},{8,10},{9,11},{10,... | collective-permute-start | bytes 688136 | tf_op jit(solution)/shard_map/ppermute | solution.py:36
  63.4 3.9 %collective-permute-done.11 = bf16[16,3584]{1,0:T(8,128)(2,1)S(1)} collective-permute-done((bf16[16,3584]{1,0:T(8,128)(2,1)S(1)}, bf16[16,3584]{1,0:T(8,128)(2,1)S(1)}, u32[]{:S(2)}, u32[]{:S(2)}) %collective-permute-start.11) | collective-permute-done | bytes 114720 | tf_op jit(solution)/shard_map/ppermute | solution.py:36
  68.3 3.9 %collective-permute-done.9 = bf16[32,3584]{1,0:T(8,128)(2,1)S(1)} collective-permute-done((bf16[32,3584]{1,0:T(8,128)(2,1)S(1)}, bf16[32,3584]{1,0:T(8,128)(2,1)S(1)}, u32[]{:S(2)}, u32[]{:S(2)}) %collective-permute-start.9) | collective-permute-done | bytes 229408 | tf_op jit(solution)/shard_map/ppermute | solution.py:36
  72.8 2.6 %collective-permute-start.13 = (bf16[16,3584]{1,0:T(8,128)(2,1)S(1)}, bf16[16,3584]{1,0:T(8,128)(2,1)S(1)}, u32[]{:S(2)}, u32[]{:S(2)}) collective-permute-start(bf16[16,3584]{1,0:T(8,128)(2,1)S(1)} %get-tuple-element.8), channel_id=1, source_target_pairs={{0,8},{1,9},{2,10},{3,11},{4,12},{5,13},{6,14},{7,15},{8,0},{9,1},... | collective-permute-start | bytes 344072 | tf_op jit(solution)/shard_map/ppermute | solution.py:36
  75.4 1.9 %collective-permute-done.10 = bf16[16,3584]{1,0:T(8,128)(2,1)S(1)} collective-permute-done((bf16[16,3584]{1,0:T(8,128)(2,1)S(1)}, bf16[16,3584]{1,0:T(8,128)(2,1)S(1)}, u32[]{:S(2)}, u32[]{:S(2)}) %collective-permute-start.10) | collective-permute-done | bytes 114720 | tf_op jit(solution)/shard_map/ppermute | solution.py:36
  77.3 2.4 %collective-permute-done.13 = bf16[16,3584]{1,0:T(8,128)(2,1)S(1)} collective-permute-done((bf16[16,3584]{1,0:T(8,128)(2,1)S(1)}, bf16[16,3584]{1,0:T(8,128)(2,1)S(1)}, u32[]{:S(2)}, u32[]{:S(2)}) %collective-permute-start.13) | collective-permute-done | bytes 114720 | tf_op jit(solution)/shard_map/ppermute | solution.py:36
  79.7 0.7 fusion.29
  (28 shorter events, 4.8 us)
Async XLA Ops:
  0.0 50.0 %copy-start = (bf16[128,3584]{1,0:T(8,128)(2,1)S(1)}, bf16[128,3584]{1,0:T(8,128)(2,1)}, u32[]{:S(2)}) copy-start(bf16[128,3584]{1,0:T(8,128)(2,1)} %param.19) | copy-start | bytes 2752516
  4.4 7.6 %collective-permute-start.1 = (bf16[16,3712]{1,0:T(8,128)(2,1)S(1)}, bf16[16,3712]{1,0:T(8,128)(2,1)S(1)}, u32[]{:S(2)}, u32[]{:S(2)}) collective-permute-start(bf16[16,3712]{1,0:T(8,128)(2,1)S(1)} %get-tuple-element.24), channel_id=1, source_target_pairs={{0,4},{1,5},{2,6},{3,7},{4,0},{5,1},{6,2},{7,3},{8,12},{9,13},{10,... | collective-permute-start | bytes 356360 | tf_op jit(solution)/shard_map/ppermute | solution.py:36
  7.4 8.2 %collective-permute-start.2 = (bf16[16,3712]{1,0:T(8,128)(2,1)S(1)}, bf16[16,3712]{1,0:T(8,128)(2,1)S(1)}, u32[]{:S(2)}, u32[]{:S(2)}) collective-permute-start(bf16[16,3712]{1,0:T(8,128)(2,1)S(1)} %get-tuple-element.24), channel_id=1, source_target_pairs={{0,8},{1,9},{2,10},{3,11},{4,12},{5,13},{6,14},{7,15},{8,0},{9,1},... | collective-permute-start | bytes 356360 | tf_op jit(solution)/shard_map/ppermute | solution.py:36
  10.0 7.7 %collective-permute-start = (bf16[16,3712]{1,0:T(8,128)(2,1)S(1)}, bf16[16,3712]{1,0:T(8,128)(2,1)S(1)}, u32[]{:S(2)}, u32[]{:S(2)}) collective-permute-start(bf16[16,3712]{1,0:T(8,128)(2,1)S(1)} %get-tuple-element.24), channel_id=1, source_target_pairs={{0,2},{1,3},{2,0},{3,1},{4,6},{5,7},{6,4},{7,5},{8,10},{9,11},{10,... | collective-permute-start | bytes 356360 | tf_op jit(solution)/shard_map/ppermute | solution.py:36
  15.7 7.6 %collective-permute-start.4 = (bf16[32,3712]{1,0:T(8,128)(2,1)S(1)}, bf16[32,3712]{1,0:T(8,128)(2,1)S(1)}, u32[]{:S(2)}, u32[]{:S(2)}) collective-permute-start(bf16[32,3712]{1,0:T(8,128)(2,1)S(1)} %pad_maximum_fusion), channel_id=1, source_target_pairs={{0,2},{1,3},{2,0},{3,1},{4,6},{5,7},{6,4},{7,5},{8,10},{9,11},{10,... | collective-permute-start | bytes 712712 | tf_op jit(solution)/shard_map/ppermute | solution.py:36
  17.2 4.8 %collective-permute-start.3 = (bf16[16,3712]{1,0:T(8,128)(2,1)S(1)}, bf16[16,3712]{1,0:T(8,128)(2,1)S(1)}, u32[]{:S(2)}, u32[]{:S(2)}) collective-permute-start(bf16[16,3712]{1,0:T(8,128)(2,1)S(1)} %collective-permute-done.2), channel_id=1, source_target_pairs={{0,4},{1,5},{2,6},{3,7},{4,0},{5,1},{6,2},{7,3},{8,12},{9,13},{10,... | collective-permute-start | bytes 356360 | tf_op jit(solution)/shard_map/ppermute | solution.py:36
  22.1 4.8 %collective-permute-start.5 = (bf16[16,3712]{1,0:T(8,128)(2,1)S(1)}, bf16[16,3712]{1,0:T(8,128)(2,1)S(1)}, u32[]{:S(2)}, u32[]{:S(2)}) collective-permute-start(bf16[16,3712]{1,0:T(8,128)(2,1)S(1)} %collective-permute-done.3), channel_id=1, source_target_pairs={{0,2},{1,3},{2,0},{3,1},{4,6},{5,7},{6,4},{7,5},{8,10},{9,11},{10,... | collective-permute-start | bytes 356360 | tf_op jit(solution)/shard_map/ppermute | solution.py:36
  27.6 2.9 %collective-permute-start.6 = (bf16[128,3712]{1,0:T(8,128)(2,1)}, bf16[128,3712]{1,0:T(8,128)(2,1)}, u32[]{:S(2)}, u32[]{:S(2)}) collective-permute-start(bf16[128,3712]{1,0:T(8,128)(2,1)} %get-tuple-element.13), channel_id=1, source_target_pairs={{0,1},{1,0},{2,3},{3,2},{4,5},{5,4},{6,7},{7,6},{8,9},{9,8},{10,11... | collective-permute-start | bytes 2850824 | tf_op jit(solution)/shard_map/ppermute | solution.py:36
  27.6 4.3 %copy-start.1 = (bf16[3584,128]{1,0:T(8,128)(2,1)S(1)}, bf16[3584,128]{1,0:T(8,128)(2,1)}, u32[]{:S(2)}) copy-start(bf16[3584,128]{1,0:T(8,128)(2,1)} %param.18) | copy-start | bytes 2752516
  56.9 2.5 %collective-permute-start.7 = (bf16[128,3584]{1,0:T(8,128)(2,1)S(1)}, bf16[128,3584]{1,0:T(8,128)(2,1)S(1)}, u32[]{:S(2)}, u32[]{:S(2)}) collective-permute-start(bf16[128,3584]{1,0:T(8,128)(2,1)S(1)} %slice.60), channel_id=1, source_target_pairs={{0,1},{1,0},{2,3},{3,2},{4,5},{5,4},{6,7},{7,6},{8,9},{9,8},{10,11... | collective-permute-start | bytes 2752520 | tf_op jit(solution)/shard_map/ppermute | solution.py:36
  61.2 6.1 %collective-permute-start.11 = (bf16[16,3584]{1,0:T(8,128)(2,1)S(1)}, bf16[16,3584]{1,0:T(8,128)(2,1)S(1)}, u32[]{:S(2)}, u32[]{:S(2)}) collective-permute-start(bf16[16,3584]{1,0:T(8,128)(2,1)S(1)} %get-tuple-element.10), channel_id=1, source_target_pairs={{0,2},{1,3},{2,0},{3,1},{4,6},{5,7},{6,4},{7,5},{8,10},{9,11},{10,... | collective-permute-start | bytes 344072 | tf_op jit(solution)/shard_map/ppermute | solution.py:36
  61.8 10.4 %collective-permute-start.9 = (bf16[32,3584]{1,0:T(8,128)(2,1)S(1)}, bf16[32,3584]{1,0:T(8,128)(2,1)S(1)}, u32[]{:S(2)}, u32[]{:S(2)}) collective-permute-start(bf16[32,3584]{1,0:T(8,128)(2,1)S(1)} %concatenate.21), channel_id=1, source_target_pairs={{0,2},{1,3},{2,0},{3,1},{4,6},{5,7},{6,4},{7,5},{8,10},{9,11},{10,... | collective-permute-start | bytes 688136 | tf_op jit(solution)/shard_map/ppermute | solution.py:36
  67.3 4.9 %collective-permute-start.12 = (bf16[16,3584]{1,0:T(8,128)(2,1)S(1)}, bf16[16,3584]{1,0:T(8,128)(2,1)S(1)}, u32[]{:S(2)}, u32[]{:S(2)}) collective-permute-start(bf16[16,3584]{1,0:T(8,128)(2,1)S(1)} %fusion.23), channel_id=1, source_target_pairs={{0,4},{1,5},{2,6},{3,7},{4,0},{5,1},{6,2},{7,3},{8,12},{9,13},{10,... | collective-permute-start | bytes 344072 | tf_op jit(solution)/shard_map/ppermute | solution.py:36
  67.8 7.6 %collective-permute-start.8 = (bf16[16,3584]{1,0:T(8,128)(2,1)S(1)}, bf16[16,3584]{1,0:T(8,128)(2,1)S(1)}, u32[]{:S(2)}, u32[]{:S(2)}) collective-permute-start(bf16[16,3584]{1,0:T(8,128)(2,1)S(1)} %get-tuple-element.9), channel_id=1, source_target_pairs={{0,2},{1,3},{2,0},{3,1},{4,6},{5,7},{6,4},{7,5},{8,10},{9,11},{10,... | collective-permute-start | bytes 344072 | tf_op jit(solution)/shard_map/ppermute | solution.py:36
  72.3 5.0 %collective-permute-start.10 = (bf16[16,3584]{1,0:T(8,128)(2,1)S(1)}, bf16[16,3584]{1,0:T(8,128)(2,1)S(1)}, u32[]{:S(2)}, u32[]{:S(2)}) collective-permute-start(bf16[16,3584]{1,0:T(8,128)(2,1)S(1)} %get-tuple-element.7), channel_id=1, source_target_pairs={{0,4},{1,5},{2,6},{3,7},{4,0},{5,1},{6,2},{7,3},{8,12},{9,13},{10,... | collective-permute-start | bytes 344072 | tf_op jit(solution)/shard_map/ppermute | solution.py:36
  72.8 6.9 %collective-permute-start.13 = (bf16[16,3584]{1,0:T(8,128)(2,1)S(1)}, bf16[16,3584]{1,0:T(8,128)(2,1)S(1)}, u32[]{:S(2)}, u32[]{:S(2)}) collective-permute-start(bf16[16,3584]{1,0:T(8,128)(2,1)S(1)} %get-tuple-element.8), channel_id=1, source_target_pairs={{0,8},{1,9},{2,10},{3,11},{4,12},{5,13},{6,14},{7,15},{8,0},{9,1},... | collective-permute-start | bytes 344072 | tf_op jit(solution)/shard_map/ppermute | solution.py:36
